TPU v7x, 256 devices: a whole 4x4x8 slice. The times are simulated.
256 devices in a mesh: tm: 32 (over z, x), height: 8 (over y, core).
Axes of the slice: x: 4, y: 4, z: 8, core: 2. Of those that a mesh axis runs over, the one named last changes fastest.
Arguments:
- latents: bfloat16 [64, 64, 104, 256], P('tm', 'height'), may hold values from -45 to 45
- first_gain: bfloat16 [256], replicated, may hold values from 0.099609375 to 1.8984375
- first_kernel: bfloat16 [3, 3, 3, 256, 256], replicated, may hold values from -0.078125 to 0.078125
- first_bias: bfloat16 [256], replicated, may hold values from -3 to 3
- second_gain: bfloat16 [256], replicated, may hold values from 0.099609375 to 1.8984375
- second_kernel: bfloat16 [3, 3, 3, 256, 256], replicated, may hold values from -0.078125 to 0.078125
- second_bias: bfloat16 [256], replicated, may hold values from -3 to 3
Outputs:
- decoded: bfloat16 [64, 64, 104, 256], P('tm', 'height')
All inputs are finite; a program needn't handle non-finite values.
Results may differ from a plain program's by a relative error of at most 0.0055.
Values may be sent and summed in bfloat16 or wider, within the bound.
A program may use at most 64 MiB of HBM per device.

v0:
```python
import jax
import jax.numpy as jnp
from jax import lax
from jax.sharding import PartitionSpec as P

EPSILON = 1e-06


def shifted(block, axis, distance):
    devices = range(lax.axis_size(axis))
    route = [(i - distance, i) for i in devices if i - distance in devices]
    return lax.ppermute(block, axis, route)


def padded_2(array, sides, width):
    for axis, dim in sides:
        peers, length = (lax.axis_size(axis), array.shape[dim])
        up = [(i, (i + 1) % peers) for i in range(peers - 1)]
        down = [(j, i) for i, j in up]
        last = lax.slice_in_dim(array, length - width, length, axis=dim)
        initial = lax.slice_in_dim(array, 0, width, axis=dim)
        before = lax.ppermute(last, axis, up)
        after = lax.ppermute(initial, axis, down)
        array = jnp.concatenate([before, array, after], axis=dim)
    return array


def activate(field, gain):
    values = field.astype(jnp.float32)
    mean_power = jnp.mean(jnp.square(values), axis=-1, keepdims=True)
    normed = values * lax.rsqrt(mean_power + EPSILON) * gain.astype(jnp.float32)
    return jax.nn.silu(normed).astype(jnp.bfloat16)


def borders(block):
    cached = shifted(block, "tm", 1)
    longer = jnp.concatenate([cached, block], 0)
    return padded_2(longer, (("height", 1),), 1)


def causal_conv(widened, kernel, bias):
    frames = widened.shape[0] - 2
    rows = widened.shape[1] - 2
    cells = widened.shape[2]
    channels = widened.shape[3]
    padded = jnp.pad(widened, ((0, 0), (0, 0), (1, 1), (0, 0)))
    total = jnp.zeros((frames * rows * cells, channels), jnp.float32)
    for tap_time in range(3):
        for tap_row in range(3):
            columns = jnp.concatenate(
                [
                    padded[
                        tap_time : tap_time + frames,
                        tap_row : tap_row + rows,
                        tap_col : tap_col + cells,
                    ]
                    for tap_col in range(3)
                ],
                -1,
            )
            columns = columns.reshape(frames * rows * cells, 3 * channels)
            taps = kernel[tap_time, tap_row].reshape(3 * channels, channels)
            total = total + jnp.dot(columns, taps, preferred_element_type=jnp.float32)
    return total.reshape(frames, rows, cells, channels) + bias.astype(jnp.float32)


def section(block, gain, kernel, bias):
    widened = borders(activate(block, gain))
    return causal_conv(widened, kernel, bias)


def per_device(
    latents, first_gain, first_kernel, first_bias, second_gain, second_kernel, second_bias
):
    first_out = section(latents, first_gain, first_kernel, first_bias).astype(jnp.bfloat16)
    second_out = section(first_out, second_gain, second_kernel, second_bias)
    return (latents.astype(jnp.float32) + second_out).astype(jnp.bfloat16)


def solution(mesh):
    return jax.shard_map(
        per_device,
        mesh=mesh,
        in_specs=(P("tm", "height", None, None), P(), P(), P(), P(), P(), P()),
        out_specs=P("tm", "height", None, None),
        check_vma=False,
    )
```

profile of v0, /device:TPU:137, one launch (start us, length us, event | category | flops | bytes accessed | tf_op | source)
XLA Modules:
  0.0 121.3 jit_solution(1120190432587362393)
XLA Ops:
  0.0 1.6 %fusion.15 = f32[2,8,104]{2,1,0:T(8,128)S(1)} fusion(bf16[2,8,104,256]{3,2,1,0:T(8,128)(2,1)} %param.7), kind=kLoop, calls=%fused_computation.60 | loop fusion | flops 1276288 | bytes 858624 | tf_op jit(solution)/shard_map/reduce_sum | solution.py:30
  1.7 0.7 convert_element_type.41
  2.3 1.7 %fusion.22 = bf16[2,8,104,256]{3,2,1,0:T(8,128)(2,1)S(1)} fusion(bf16[2,8,104,256]{3,2,1,0:T(8,128)(2,1)} %param.7, f32[256]{0:T(256)S(1)} %convert_element_type.41, f32[2,8,104]{2,1,0:T(8,128)S(1)} %add_rsqrt_fusion.1), kind=kLoop, calls=%fused_computation.67 | loop fusion | flops 3407872 | bytes 1711616 | tf_op jit(solution)/shard_map/convert_element_type | solution.py:32
  4.1 3.1 %collective-permute-start = (bf16[2,8,104,256]{3,2,1,0:T(8,128)(2,1)S(1)}, bf16[2,8,104,256]{3,2,1,0:T(8,128)(2,1)S(1)}, u32[]{:S(2)}, u32[]{:S(2)}) collective-permute-start(bf16[2,8,104,256]{3,2,1,0:T(8,128)(2,1)S(1)} %fusion.22), channel_id=1, source_target_pairs={{0,8},{8,16},{16,24},{24,32},{32,40},{40,48},{48,56},{56,64},{64,7... | collective-permute-start | bytes 2555912 | tf_op jit(solution)/shard_map/ppermute | solution.py:12
  7.2 21.9 %collective-permute-done = bf16[2,8,104,256]{3,2,1,0:T(8,128)(2,1)S(1)} collective-permute-done((bf16[2,8,104,256]{3,2,1,0:T(8,128)(2,1)S(1)}, bf16[2,8,104,256]{3,2,1,0:T(8,128)(2,1)S(1)}, u32[]{:S(2)}, u32[]{:S(2)}) %collective-permute-start) | collective-permute-done | bytes 852000 | tf_op jit(solution)/shard_map/ppermute | solution.py:12
  29.1 4.6 %collective-permute-start.1 = (bf16[4,1,104,256]{3,2,1,0:T(8,128)(2,1)S(1)}, bf16[4,1,104,256]{3,2,1,0:T(8,128)(2,1)S(1)}, u32[]{:S(2)}, u32[]{:S(2)}) collective-permute-start(bf16[4,1,104,256]{3,2,1,0:T(8,128)(2,1)S(1)} %get-tuple-element.77), channel_id=1, source_target_pairs={{0,1},{1,2},{2,3},{3,4},{4,5},{5,6},{6,7},{8,9},{9,10},{10,11},{11... | collective-permute-start | bytes 638984 | tf_op jit(solution)/shard_map/ppermute | solution.py:22
  33.8 1.9 %collective-permute-start.2 = (bf16[4,1,104,256]{3,2,1,0:T(8,128)(2,1)S(1)}, bf16[4,1,104,256]{3,2,1,0:T(8,128)(2,1)S(1)}, u32[]{:S(2)}, u32[]{:S(2)}) collective-permute-start(bf16[4,1,104,256]{3,2,1,0:T(8,128)(2,1)S(1)} %get-tuple-element.78), channel_id=1, source_target_pairs={{1,0},{2,1},{3,2},{4,3},{5,4},{6,5},{7,6},{9,8},{10,9},{11,10},{12... | collective-permute-start | bytes 638984 | tf_op jit(solution)/shard_map/ppermute | solution.py:23
  35.7 1.7 %fusion.25 = (bf16[1,1,3,256,256]{4,3,2,1,0:T(8,128)(2,1)S(1)}, bf16[1,1,3,256,256]{4,3,2,1,0:T(8,128)(2,1)}, bf16[1,1,3,256,256]{4,3,2,1,0:T(8,128)(2,1)}, bf16...) fusion(bf16[3,3,3,256,256]{4,3,2,1,0:T(8,128)(2,1)S(1)} %copy-d, ...), kind=kLoop, calls=%fused_computation.80 | loop fusion | bytes 7077888 | tf_op jit(solution)/shard_map/slice | solution.py:62
  37.4 3.5 %collective-permute-done.2 = bf16[4,1,104,256]{3,2,1,0:T(8,128)(2,1)S(1)} collective-permute-done((bf16[4,1,104,256]{3,2,1,0:T(8,128)(2,1)S(1)}, bf16[4,1,104,256]{3,2,1,0:T(8,128)(2,1)S(1)}, u32[]{:S(2)}, u32[]{:S(2)}) %collective-permute-start.2) | collective-permute-done | bytes 213024 | tf_op jit(solution)/shard_map/ppermute | solution.py:23
  40.9 1.0 fusion.12
  41.9 5.5 %fusion.27 = (bf16[2,8,104,256]{3,2,1,0:T(8,128)(2,1)S(1)}, bf16[2,8,104,256]{3,2,1,0:T(8,128)(2,1)S(1)}, bf16[2,8,104,256]{3,2,1,0:T(8,128)(2,1)S(1)}, bf16[2,8...) fusion(bf16[4,10,106,256]{3,2,1,0:T(8,128)(2,1)S(1)} %fusion.12), kind=kLoop, calls=%fused_computation.82 | loop fusion | bytes 30670848 | tf_op jit(solution)/shard_map/slice | solution.py:52
  47.4 0.9 pad_maximum_fusion.18
  48.9 0.8 copy-done.21
  49.7 0.8 fusion.32
  50.6 1.0 pad_maximum_fusion.8
  51.6 0.9 convolution_add_fusion.15
  52.7 0.8 copy-done.19
  53.5 0.8 convolution_add_fusion.14
  54.5 0.8 copy-done.18
  55.3 0.8 convolution_add_fusion.13
  56.3 0.9 convolution_add_fusion.12
  57.4 0.8 copy-done.15
  58.2 0.8 convolution_add_fusion.11
  59.2 0.8 copy-done.12
  60.1 0.8 convolution_add_fusion.10
  61.1 0.9 convolution_add_fusion.9
  62.1 0.9 multiply_reduce_fusion
  63.8 2.1 %collective-permute-start.3 = (bf16[2,8,104,256]{3,2,1,0:T(8,128)(2,1)S(1)}, bf16[2,8,104,256]{3,2,1,0:T(8,128)(2,1)S(1)}, u32[]{:S(2)}, u32[]{:S(2)}) collective-permute-start(bf16[2,8,104,256]{3,2,1,0:T(8,128)(2,1)S(1)} %multiply_convert_fusion), channel_id=1, source_target_pairs={{0,8},{8,16},{16,24},{24,32},{32,40},{40,48},{48,56},{56,64},{64,7... | collective-permute-start | bytes 2555912 | tf_op jit(solution)/shard_map/ppermute | solution.py:12
  65.8 23.1 %collective-permute-done.3 = bf16[2,8,104,256]{3,2,1,0:T(8,128)(2,1)S(1)} collective-permute-done((bf16[2,8,104,256]{3,2,1,0:T(8,128)(2,1)S(1)}, bf16[2,8,104,256]{3,2,1,0:T(8,128)(2,1)S(1)}, u32[]{:S(2)}, u32[]{:S(2)}) %collective-permute-start.3) | collective-permute-done | bytes 852000 | tf_op jit(solution)/shard_map/ppermute | solution.py:12
  88.9 3.2 %collective-permute-start.4 = (bf16[4,1,104,256]{3,2,1,0:T(8,128)(2,1)S(1)}, bf16[4,1,104,256]{3,2,1,0:T(8,128)(2,1)S(1)}, u32[]{:S(2)}, u32[]{:S(2)}) collective-permute-start(bf16[4,1,104,256]{3,2,1,0:T(8,128)(2,1)S(1)} %get-tuple-element.73), channel_id=1, source_target_pairs={{0,1},{1,2},{2,3},{3,4},{4,5},{5,6},{6,7},{8,9},{9,10},{10,11},{11... | collective-permute-start | bytes 638984 | tf_op jit(solution)/shard_map/ppermute | solution.py:22
  92.2 1.9 %collective-permute-start.5 = (bf16[4,1,104,256]{3,2,1,0:T(8,128)(2,1)S(1)}, bf16[4,1,104,256]{3,2,1,0:T(8,128)(2,1)S(1)}, u32[]{:S(2)}, u32[]{:S(2)}) collective-permute-start(bf16[4,1,104,256]{3,2,1,0:T(8,128)(2,1)S(1)} %get-tuple-element.74), channel_id=1, source_target_pairs={{1,0},{2,1},{3,2},{4,3},{5,4},{6,5},{7,6},{9,8},{10,9},{11,10},{12... | collective-permute-start | bytes 638984 | tf_op jit(solution)/shard_map/ppermute | solution.py:23
  94.1 1.6 %fusion.24 = (bf16[1,1,3,256,256]{4,3,2,1,0:T(8,128)(2,1)S(1)}, bf16[1,1,3,256,256]{4,3,2,1,0:T(8,128)(2,1)}, bf16[1,1,3,256,256]{4,3,2,1,0:T(8,128)(2,1)}, bf16...) fusion(bf16[3,3,3,256,256]{4,3,2,1,0:T(8,128)(2,1)S(1)} %copy-d, ...), kind=kLoop, calls=%fused_computation.79 | loop fusion | bytes 7077888 | tf_op jit(solution)/shard_map/slice | solution.py:62
  95.7 3.6 %collective-permute-done.5 = bf16[4,1,104,256]{3,2,1,0:T(8,128)(2,1)S(1)} collective-permute-done((bf16[4,1,104,256]{3,2,1,0:T(8,128)(2,1)S(1)}, bf16[4,1,104,256]{3,2,1,0:T(8,128)(2,1)S(1)}, u32[]{:S(2)}, u32[]{:S(2)}) %collective-permute-start.5) | collective-permute-done | bytes 213024 | tf_op jit(solution)/shard_map/ppermute | solution.py:23
  99.4 0.9 pad_maximum_fusion.19
  100.4 1.0 select_maximum_fusion
  101.4 5.8 %fusion.26 = (bf16[2,8,104,256]{3,2,1,0:T(8,128)(2,1)}, bf16[2,8,104,256]{3,2,1,0:T(8,128)(2,1)S(1)}, bf16[2,8,104,256]{3,2,1,0:T(8,128)(2,1)S(1)}, bf16[2,8,104...) fusion(bf16[4,10,106,256]{3,2,1,0:T(8,128)(2,1)S(1)} %select_ma, ...), kind=kLoop, calls=%fused_computation.81 | loop fusion | bytes 30670848 | tf_op jit(solution)/shard_map/slice | solution.py:52
  107.6 0.8 fusion.33
  109.2 1.0 copy-done.3
  111.1 1.0 pad_maximum_fusion.16
  112.2 0.8 convolution_add_fusion.7
  113.2 0.8 convolution_add_fusion.6
  114.2 0.8 convolution_add_fusion.5
  115.2 0.8 convolution_add_fusion.4
  116.2 0.9 convolution_add_fusion.3
  117.1 0.9 convolution_add_fusion.2
  118.1 0.8 convolution_add_fusion.1
  119.0 0.9 convolution_add_fusion
  120.1 1.1 fusion.23
  (70 shorter events, 5.7 us)
Async XLA Ops:
  0.0 7.2 %copy-start.22 = (bf16[256]{0:T(256)(128)(2,1)S(1)}, bf16[256]{0:T(256)(128)(2,1)}, u32[]{:S(2)}) copy-start(bf16[256]{0:T(256)(128)(2,1)} %param.10) | copy-start | bytes 1540
  0.0 7.2 %copy-start.23 = (bf16[256]{0:T(256)(128)(2,1)S(1)}, bf16[256]{0:T(256)(128)(2,1)}, u32[]{:S(2)}) copy-start(bf16[256]{0:T(256)(128)(2,1)} %param.11) | copy-start | bytes 1540
  0.0 35.7 %copy-start.1 = (bf16[3,3,3,256,256]{4,3,2,1,0:T(8,128)(2,1)S(1)}, bf16[3,3,3,256,256]{4,3,2,1,0:T(8,128)(2,1)}, u32[]{:S(2)}) copy-start(bf16[3,3,3,256,256]{4,3,2,1,0:T(8,128)(2,1)} %param.9) | copy-start | bytes 10616836
  4.1 25.0 %collective-permute-start = (bf16[2,8,104,256]{3,2,1,0:T(8,128)(2,1)S(1)}, bf16[2,8,104,256]{3,2,1,0:T(8,128)(2,1)S(1)}, u32[]{:S(2)}, u32[]{:S(2)}) collective-permute-start(bf16[2,8,104,256]{3,2,1,0:T(8,128)(2,1)S(1)} %fusion.22), channel_id=1, source_target_pairs={{0,8},{8,16},{16,24},{24,32},{32,40},{40,48},{48,56},{56,64},{64,7... | collective-permute-start | bytes 2555912 | tf_op jit(solution)/shard_map/ppermute | solution.py:12
  29.1 8.3 %collective-permute-start.1 = (bf16[4,1,104,256]{3,2,1,0:T(8,128)(2,1)S(1)}, bf16[4,1,104,256]{3,2,1,0:T(8,128)(2,1)S(1)}, u32[]{:S(2)}, u32[]{:S(2)}) collective-permute-start(bf16[4,1,104,256]{3,2,1,0:T(8,128)(2,1)S(1)} %get-tuple-element.77), channel_id=1, source_target_pairs={{0,1},{1,2},{2,3},{3,4},{4,5},{5,6},{6,7},{8,9},{9,10},{10,11},{11... | collective-permute-start | bytes 638984 | tf_op jit(solution)/shard_map/ppermute | solution.py:22
  33.8 7.2 %collective-permute-start.2 = (bf16[4,1,104,256]{3,2,1,0:T(8,128)(2,1)S(1)}, bf16[4,1,104,256]{3,2,1,0:T(8,128)(2,1)S(1)}, u32[]{:S(2)}, u32[]{:S(2)}) collective-permute-start(bf16[4,1,104,256]{3,2,1,0:T(8,128)(2,1)S(1)} %get-tuple-element.78), channel_id=1, source_target_pairs={{1,0},{2,1},{3,2},{4,3},{5,4},{6,5},{7,6},{9,8},{10,9},{11,10},{12... | collective-permute-start | bytes 638984 | tf_op jit(solution)/shard_map/ppermute | solution.py:23
  48.7 1.0 copy-start.21
  50.6 1.0 copy-start.20
  52.5 1.0 copy-start.19
  54.3 1.0 copy-start.18
  55.3 1.0 copy-start.17
  57.2 1.0 copy-start.15
  59.1 1.0 copy-start.12
  60.1 1.0 copy-start.10
  63.1 2.8 %copy-start.24 = (bf16[256]{0:T(256)(128)(2,1)S(1)}, bf16[256]{0:T(256)(128)(2,1)}, u32[]{:S(2)}) copy-start(bf16[256]{0:T(256)(128)(2,1)} %param.13) | copy-start | bytes 1540
  63.2 30.9 %copy-start.2 = (bf16[3,3,3,256,256]{4,3,2,1,0:T(8,128)(2,1)S(1)}, bf16[3,3,3,256,256]{4,3,2,1,0:T(8,128)(2,1)}, u32[]{:S(2)}) copy-start(bf16[3,3,3,256,256]{4,3,2,1,0:T(8,128)(2,1)} %param.12) | copy-start | bytes 10616836
  63.8 25.1 %collective-permute-start.3 = (bf16[2,8,104,256]{3,2,1,0:T(8,128)(2,1)S(1)}, bf16[2,8,104,256]{3,2,1,0:T(8,128)(2,1)S(1)}, u32[]{:S(2)}, u32[]{:S(2)}) collective-permute-start(bf16[2,8,104,256]{3,2,1,0:T(8,128)(2,1)S(1)} %multiply_convert_fusion), channel_id=1, source_target_pairs={{0,8},{8,16},{16,24},{24,32},{32,40},{40,48},{48,56},{56,64},{64,7... | collective-permute-start | bytes 2555912 | tf_op jit(solution)/shard_map/ppermute | solution.py:12
  88.9 6.8 %collective-permute-start.4 = (bf16[4,1,104,256]{3,2,1,0:T(8,128)(2,1)S(1)}, bf16[4,1,104,256]{3,2,1,0:T(8,128)(2,1)S(1)}, u32[]{:S(2)}, u32[]{:S(2)}) collective-permute-start(bf16[4,1,104,256]{3,2,1,0:T(8,128)(2,1)S(1)} %get-tuple-element.73), channel_id=1, source_target_pairs={{0,1},{1,2},{2,3},{3,4},{4,5},{5,6},{6,7},{8,9},{9,10},{10,11},{11... | collective-permute-start | bytes 638984 | tf_op jit(solution)/shard_map/ppermute | solution.py:22
  92.2 7.2 %collective-permute-start.5 = (bf16[4,1,104,256]{3,2,1,0:T(8,128)(2,1)S(1)}, bf16[4,1,104,256]{3,2,1,0:T(8,128)(2,1)S(1)}, u32[]{:S(2)}, u32[]{:S(2)}) collective-permute-start(bf16[4,1,104,256]{3,2,1,0:T(8,128)(2,1)S(1)} %get-tuple-element.74), channel_id=1, source_target_pairs={{1,0},{2,1},{3,2},{4,3},{5,4},{6,5},{7,6},{9,8},{10,9},{11,10},{12... | collective-permute-start | bytes 638984 | tf_op jit(solution)/shard_map/ppermute | solution.py:23
  107.6 1.2 copy-start.5
  107.6 1.4 %copy-start.6 = (bf16[2,8,104,256]{3,2,1,0:T(8,128)(2,1)S(1)}, bf16[2,8,104,256]{3,2,1,0:T(8,128)(2,1)}, u32[]{:S(2)}) copy-start(bf16[2,8,104,256]{3,2,1,0:T(8,128)(2,1)} %get-tuple-element.40) | copy-start | bytes 2555908
  109.0 1.2 copy-start.3
  109.0 1.4 %copy-start.4 = (bf16[2,8,104,256]{3,2,1,0:T(8,128)(2,1)S(1)}, bf16[2,8,104,256]{3,2,1,0:T(8,128)(2,1)}, u32[]{:S(2)}) copy-start(bf16[2,8,104,256]{3,2,1,0:T(8,128)(2,1)} %get-tuple-element.27) | copy-start | bytes 2555908
  111.1 1.0 copy-start.16
  112.2 1.0 copy-start.14
  113.2 1.0 copy-start.13
  114.2 1.0 copy-start.11
  115.2 1.0 copy-start.9
  116.2 1.0 copy-start.8
  117.1 1.0 copy-start.7
  119.0 1.2 copy-start
where the time goes:
time: 122 us; the launch traced here: 121 us
  waiting for transfers between devices  52.1 us (43%)
  local copies, waits for them, and re-layouts  22.7 us (19%)
  starting transfers between devices  16.9 us (14%)
  matrix products  15.5 us (13%)
  other arithmetic  13.5 us (11%)
    ppermute x2, waiting for transfers between devices, shifted(): return lax.ppermute(block, axis, route)  44.9 us
    dot_general x18, matrix products, causal_conv(): total = total + jnp.dot(columns, taps, preferred_element_type=jnp.float32)  15.5 us
    slice x5, local copies, waits for them, and re-layouts, causal_conv(): padded[tap_time:tap_time + frames, tap_row:tap_row + rows, tap_col:tap_co...  12.1 us
    ppermute x2, starting transfers between devices, padded_2(): before = lax.ppermute(last, axis, up)  7.88 us
    unnamed x50, local copies, waits for them, and re-layouts  7.28 us
    ppermute x2, waiting for transfers between devices, padded_2(): after = lax.ppermute(initial, axis, down)  7.15 us
    ppermute x2, starting transfers between devices, shifted(): return lax.ppermute(block, axis, route)  5.17 us
    concatenate x14, other arithmetic, causal_conv(): jnp.concatenate([padded[tap_time:tap_time + frames, tap_row:tap_row + row...  3.98 us
  transfers between devices with their start and end apart: 6, of which 4 were waited for; matrix products, arithmetic and copies ran while one was open for 3% of the time, Pallas kernels for 0%

commit v1 on v0

v1 whole, which is shorter than its diff:
```python
import functools

import jax
import jax.numpy as jnp
from jax import lax
from jax.experimental import pallas as pl
from jax.experimental.pallas import tpu as pltpu
from jax.sharding import PartitionSpec as P

EPSILON = 1e-06
MESH = pl.DeviceIdType.MESH
F32 = jnp.float32


def kernel(
    tm_size, height_size,
    lat, gain1, gain2, bias1, bias2, w1_hbm, w2_hbm,
    out,
    latv, w1, w2, halo, ledge, sendbuf, lhs, acc, outv,
    load_sem, out_sem, tm_send, tm_recv, hl_send, hl_recv, hf_send, hf_recv,
):
    frames, rows, cells, channels = latv.shape
    wide = lhs.shape[3]
    tm = lax.axis_index("tm")
    ht = lax.axis_index("height")
    has_prev = tm > 0
    has_next = tm < tm_size - 1
    has_up = ht > 0
    has_down = ht < height_size - 1

    load_lat = pltpu.make_async_copy(lat, latv, load_sem.at[0])
    load_w1 = pltpu.make_async_copy(w1_hbm, w1, load_sem.at[1])
    load_w2 = pltpu.make_async_copy(w2_hbm, w2, load_sem.at[2])
    load_lat.start()
    load_w1.start()
    load_w2.start()

    nxt = jnp.minimum(tm + 1, tm_size - 1)
    prv = jnp.maximum(tm - 1, 0)
    up = jnp.maximum(ht - 1, 0)
    down = jnp.minimum(ht + 1, height_size - 1)

    barrier = pltpu.get_barrier_semaphore()
    for exists, there in (
        (has_prev, {"tm": prv}), (has_next, {"tm": nxt}),
        (has_up, {"height": up}), (has_down, {"height": down}),
    ):
        @pl.when(exists)
        def _(there=there):
            pl.semaphore_signal(barrier, inc=1, device_id=there, device_id_type=MESH)
    peers = sum(h.astype(jnp.int32) for h in (has_prev, has_next, has_up, has_down))
    pl.semaphore_wait(barrier, peers)

    def source(e, row):
        return lat.at[:, row] if e == 0 else sendbuf.at[row]

    def tm_copy(e, row):
        return pltpu.make_async_remote_copy(
            src_ref=source(e, row), dst_ref=halo.at[e, row + 1],
            send_sem=tm_send.at[e, row], recv_sem=tm_recv.at[e, row],
            device_id={"tm": nxt}, device_id_type=MESH)

    def local_edge(e, side):
        return pltpu.make_async_remote_copy(
            src_ref=source(e, 0 if side == 0 else rows - 1), dst_ref=ledge.at[e, side],
            send_sem=hl_send.at[e, side], recv_sem=hl_recv.at[e, side],
            device_id={"height": up if side == 0 else down}, device_id_type=MESH)

    def halo_edge(e, side):
        return pltpu.make_async_remote_copy(
            src_ref=halo.at[e, 1 if side == 0 else rows],
            dst_ref=halo.at[e, rows + 1 if side == 0 else 0],
            send_sem=hf_send.at[e, side], recv_sem=hf_recv.at[e, side],
            device_id={"height": up if side == 0 else down}, device_id_type=MESH)

    to_side = (has_up, has_down)
    from_side = (has_down, has_up)

    def start_tm(e, row):
        @pl.when(has_next)
        def _():
            tm_copy(e, row).start()

    def start_local_edge(e, side):
        @pl.when(to_side[side])
        def _():
            local_edge(e, side).start()

    start_local_edge(0, 0)
    start_local_edge(0, 1)

    def send_row(i, carry):
        start_tm(0, lax.rem(i + rows - 1, rows))
        return carry

    lax.fori_loop(0, rows, send_row, 0)

    g1 = gain1[...].astype(F32)
    g2 = gain2[...].astype(F32)
    b1 = bias1[...].astype(F32)
    b2 = bias2[...].astype(F32)

    def activate(values, gain):
        power = jnp.mean(jnp.square(values), axis=-1, keepdims=True)
        return jax.nn.silu(values * lax.rsqrt(power + EPSILON) * gain)

    pad = jnp.zeros((wide - cells, channels), F32)

    def expand(e, frame, row, values):
        v = jnp.concatenate([values, pad], 0)
        lhs[e, frame, row, :, :channels] = pltpu.roll(v, 1, 0).astype(jnp.bfloat16)
        lhs[e, frame, row, :, channels:2 * channels] = v.astype(jnp.bfloat16)
        lhs[e, frame, row, :, 2 * channels:] = pltpu.roll(v, wide - 1, 0).astype(jnp.bfloat16)

    def clear(e, frame, row):
        lhs[e, frame, row] = jnp.zeros((wide, 3 * channels), jnp.bfloat16)

    def take(e, frame, row, raw):
        values = raw.astype(F32)
        if e == 0:
            values = activate(values, g1)
        expand(e, frame, row, values)

    def take_halo(e, row):
        @pl.when(has_prev)
        def _():
            tm_copy(e, row).wait_recv()
        for side, edge in ((0, 0), (1, rows - 1)):
            if isinstance(row, int) and row == edge:
                @pl.when(has_prev & to_side[side])
                def _(side=side):
                    halo_edge(e, side).start()

        @pl.when(has_prev)
        def _():
            for f in range(2):
                take(e, f, row + 1, halo[e, row + 1, f])

        @pl.when(jnp.logical_not(has_prev))
        def _():
            for f in range(2):
                clear(e, f, row + 1)

    def take_halo_edge(e, side):
        row = rows + 1 if side == 0 else 0
        there = has_prev & from_side[side]

        @pl.when(there)
        def _():
            halo_edge(e, side).wait_recv()
            for f in range(2):
                take(e, f, row, halo[e, row, f])

        @pl.when(jnp.logical_not(there))
        def _():
            for f in range(2):
                clear(e, f, row)

    def take_local_edge(e, side):
        row = rows + 1 if side == 0 else 0

        @pl.when(from_side[side])
        def _():
            local_edge(e, side).wait_recv()
            for f in range(2):
                take(e, 2 + f, row, ledge[e, side, f])

        @pl.when(jnp.logical_not(from_side[side]))
        def _():
            for f in range(2):
                clear(e, 2 + f, row)

    def tap(e, w, frame, row, count, i, j):
        block = lhs[e, frame, pl.ds(row + j, count)].reshape(count * wide, 3 * channels)
        return jnp.dot(block, w[i * 3 + j], preferred_element_type=F32)

    def local_conv(e, w, count):
        def chunk(c, carry):
            row = c * count
            first = sum(tap(e, w, 2, row, count, 2, j) for j in range(3))
            acc[e, 0, pl.ds(row, count)] = first.reshape(count, wide, channels)
            second = sum(
                tap(e, w, 2, row, count, 1, j) + tap(e, w, 3, row, count, 2, j) for j in range(3))
            acc[e, 1, pl.ds(row, count)] = second.reshape(count, wide, channels)
            return carry
        lax.fori_loop(0, rows // count, chunk, 0)

    def halo_conv(e, w, row):
        first = acc[e, 0, row] + sum(
            tap(e, w, 0, row, 1, 0, j) + tap(e, w, 1, row, 1, 1, j) for j in range(3))
        second = acc[e, 1, row] + sum(tap(e, w, 1, row, 1, 0, j) for j in range(3))
        return first[:cells], second[:cells]

    load_lat.wait()

    def own_row(row, carry):
        for f in range(2):
            take(0, 2 + f, row + 1, latv[f, row])
        return carry

    lax.fori_loop(0, rows, own_row, 0)
    take_local_edge(0, 0)
    take_local_edge(0, 1)
    load_w1.wait()
    local_conv(0, w1, 4)

    def middle_row(row):
        for f, v in enumerate(halo_conv(0, w1, row)):
            a = activate((v + b1).astype(jnp.bfloat16).astype(F32), g2)
            sendbuf[row, f] = a.astype(jnp.bfloat16)
            expand(1, 2 + f, row + 1, a)

    take_halo(0, rows - 1)
    take_halo(0, 0)
    take_halo_edge(0, 0)
    take_halo_edge(0, 1)

    def middle_step(r, carry):
        take_halo(0, r)
        middle_row(r - 1)

        @pl.when(r > 1)
        def _():
            start_tm(1, r - 2)
        return carry

    lax.fori_loop(1, rows - 2, middle_step, 0)
    start_local_edge(1, 0)
    take_halo(0, rows - 2)
    start_tm(1, rows - 4)
    middle_row(rows - 1)
    middle_row(rows - 3)
    start_tm(1, rows - 1)
    start_local_edge(1, 1)
    middle_row(rows - 2)
    start_tm(1, rows - 3)
    take_local_edge(1, 0)
    start_tm(1, rows - 2)
    take_local_edge(1, 1)
    load_w2.wait()
    local_conv(1, w2, 4)

    def out_copy(row):
        return pltpu.make_async_copy(outv.at[:, row], out.at[:, row], out_sem.at[row])

    def last_row(row):
        for f, v in enumerate(halo_conv(1, w2, row)):
            outv[f, row] = (latv[f, row].astype(F32) + (v + b2)).astype(jnp.bfloat16)
        out_copy(row).start()

    take_halo(1, 0)

    def last_step(r, carry):
        take_halo(1, r)

        @pl.when(r > 1)
        def _():
            last_row(r - 1)
        return carry

    lax.fori_loop(1, rows - 3, last_step, 0)
    take_halo(1, rows - 1)
    take_halo(1, rows - 3)
    last_row(rows - 4)
    take_halo_edge(1, 1)
    last_row(0)
    take_halo_edge(1, 0)
    take_halo(1, rows - 2)
    last_row(rows - 3)
    last_row(rows - 2)
    last_row(rows - 1)

    def drain(row, carry):
        out_copy(row).wait()

        @pl.when(has_next)
        def _():
            tm_copy(0, row).wait_send()
            tm_copy(1, row).wait_send()
        return carry

    lax.fori_loop(0, rows, drain, 0)
    for e in range(2):
        for side in range(2):
            @pl.when(to_side[side])
            def _(e=e, side=side):
                local_edge(e, side).wait_send()

            @pl.when(has_prev & to_side[side])
            def _(e=e, side=side):
                halo_edge(e, side).wait_send()


def per_device(
    tm_size, height_size,
    latents, first_gain, first_kernel, first_bias, second_gain, second_kernel, second_bias,
):
    frames, rows, cells, channels = latents.shape
    wide = -(-(cells + 1) // 16) * 16
    vmem = pl.BlockSpec(memory_space=pltpu.VMEM)
    hbm = pl.BlockSpec(memory_space=pl.ANY)
    bf16 = jnp.bfloat16
    dma = pltpu.SemaphoreType.DMA
    row = lambda v: v.reshape(1, channels)
    taps = lambda k: k.reshape(9, 3 * channels, channels)
    return pl.pallas_call(
        functools.partial(kernel, tm_size, height_size),
        out_shape=jax.ShapeDtypeStruct(latents.shape, bf16),
        in_specs=[hbm, vmem, vmem, vmem, vmem, hbm, hbm],
        out_specs=hbm,
        scratch_shapes=[
            pltpu.VMEM(latents.shape, bf16),
            pltpu.VMEM((9, 3 * channels, channels), bf16),
            pltpu.VMEM((9, 3 * channels, channels), bf16),
            pltpu.VMEM((2, rows + 2, 2, cells, channels), bf16),
            pltpu.VMEM((2, 2, 2, cells, channels), bf16),
            pltpu.VMEM((rows, 2, cells, channels), bf16),
            pltpu.VMEM((2, 4, rows + 2, wide, 3 * channels), bf16),
            pltpu.VMEM((2, 2, rows, wide, channels), F32),
            pltpu.VMEM(latents.shape, bf16),
            dma((3,)), dma((rows,)),
            dma((2, rows)), dma((2, rows)),
            dma((2, 2)), dma((2, 2)), dma((2, 2)), dma((2, 2)),
        ],
        compiler_params=pltpu.CompilerParams(
            collective_id=0, has_side_effects=True, vmem_limit_bytes=60 * 1024 * 1024),
        name="residual_block",
    )(latents, row(first_gain), row(second_gain), row(first_bias), row(second_bias),
      taps(first_kernel), taps(second_kernel))


def solution(mesh):
    return jax.shard_map(
        functools.partial(per_device, mesh.shape["tm"], mesh.shape["height"]),
        mesh=mesh,
        in_specs=(P("tm", "height", None, None), P(), P(), P(), P(), P(), P()),
        out_specs=P("tm", "height", None, None),
        check_vma=False,
    )
```

time: 122 us -> 53.8 us (0.44)
  the two profiles are of different devices: /device:TPU:137 before, /device:TPU:225 now
where the time goes in v1:
time: 53.8 us; the launch traced here: 53.2 us
  Pallas kernels  46.2 us (86%)
  local copies, waits for them, and re-layouts  6.99 us (13%)
    pallas_call x1, Pallas kernels, per_device(): pl.pallas_call(functools.partial(kernel, tm_size, height_size), out_shape...  46.2 us
    reshape x4, local copies, waits for them, and re-layouts, per_device(): row = lambda v: v.reshape(1, channels)  4.88 us
    unnamed x1, local copies, waits for them, and re-layouts  2.11 us

profile of v1, /device:TPU:225, one launch (start us, length us, event | category | flops | bytes accessed | tf_op | source)
XLA Modules:
  0.0 53.2 jit_solution(15437382208796988099)
XLA Ops:
  0.0 1.2 %reshape.18.gain1 = bf16[1,256]{1,0:T(2,128)(2,1)} reshape(bf16[256]{0:T(256)(128)(2,1)} %param.8) | data formatting | bytes 1024 | tf_op jit(solution)/shard_map/reshape | solution.py:304
  1.2 1.2 %reshape.20.bias1 = bf16[1,256]{1,0:T(2,128)(2,1)} reshape(bf16[256]{0:T(256)(128)(2,1)} %param.10) | data formatting | bytes 1024 | tf_op jit(solution)/shard_map/reshape | solution.py:304
  2.4 1.2 %reshape.19.gain2 = bf16[1,256]{1,0:T(2,128)(2,1)} reshape(bf16[256]{0:T(256)(128)(2,1)} %param.11) | data formatting | bytes 1024 | tf_op jit(solution)/shard_map/reshape | solution.py:304
  3.6 1.2 %reshape.21.bias2 = bf16[1,256]{1,0:T(2,128)(2,1)} reshape(bf16[256]{0:T(256)(128)(2,1)} %param.13) | data formatting | bytes 1024 | tf_op jit(solution)/shard_map/reshape | solution.py:304
  4.9 46.2 %residual_block.1 = bf16[2,8,104,256]{3,2,1,0:T(8,128)(2,1)} custom-call(bf16[2,8,104,256]{3,2,1,0:T(8,128)(2,1)} %lat.1, bf16[1,256]{1,0:T(2,128)(2,1)} %reshape.18.gain1, bf16[1,256]{1,0:T(2,128)(2,1)} %reshape.19.gain2, bf16[1,256]{1,0:T(2,128)(2,1)} %reshape.20.bias1, bf16[1,256]{1,0:T(2,128)(2,1)} %reshape.21.bias2, bf16[9,768,256]{2,1,0:T(8,128)(2,1)} %bitcast.2, ...), custom_call_target="tpu_custom_call" | custom-call | tf_op jit(solution)/shard_map/residual_block/pallas_call | solution.py:306
  51.1 2.1 %copy.9 = bf16[2,8,104,256]{3,2,1,0:T(8,128)(2,1)} copy(bf16[2,8,104,256]{3,2,1,0:T(8,128)(2,1)} %residual_block.1) | data formatting | bytes 1703936

commit v2 on v1

--- a/solution.py
+++ b/solution.py
@@ -16,8 +16,8 @@
     tm_size, height_size,
     lat, gain1, gain2, bias1, bias2, w1_hbm, w2_hbm,
     out,
-    latv, w1, w2, halo, ledge, sendbuf, lhs, acc, outv,
-    load_sem, out_sem, tm_send, tm_recv, hl_send, hl_recv, hf_send, hf_recv,
+    latv, w1, w2, halo, ledge, sendbuf, lhs, acc,
+    load_sem, tm_send, tm_recv, hl_send, hl_recv, hf_send, hf_recv,
 ):
     frames, rows, cells, channels = latv.shape
     wide = lhs.shape[3]
@@ -95,10 +95,10 @@
 
     lax.fori_loop(0, rows, send_row, 0)
 
-    g1 = gain1[...].astype(F32)
-    g2 = gain2[...].astype(F32)
-    b1 = bias1[...].astype(F32)
-    b2 = bias2[...].astype(F32)
+    g1 = gain1[...].astype(F32).reshape(1, channels)
+    g2 = gain2[...].astype(F32).reshape(1, channels)
+    b1 = bias1[...].astype(F32).reshape(1, channels)
+    b2 = bias2[...].astype(F32).reshape(1, channels)
 
     def activate(values, gain):
         power = jnp.mean(jnp.square(values), axis=-1, keepdims=True)
@@ -240,13 +240,9 @@
     load_w2.wait()
     local_conv(1, w2, 4)
 
-    def out_copy(row):
-        return pltpu.make_async_copy(outv.at[:, row], out.at[:, row], out_sem.at[row])
-
     def last_row(row):
         for f, v in enumerate(halo_conv(1, w2, row)):
-            outv[f, row] = (latv[f, row].astype(F32) + (v + b2)).astype(jnp.bfloat16)
-        out_copy(row).start()
+            out[f, row] = (latv[f, row].astype(F32) + (v + b2)).astype(jnp.bfloat16)
 
     take_halo(1, 0)
 
@@ -271,8 +267,6 @@
     last_row(rows - 1)
 
     def drain(row, carry):
-        out_copy(row).wait()
-
         @pl.when(has_next)
         def _():
             tm_copy(0, row).wait_send()
@@ -298,16 +292,15 @@
     frames, rows, cells, channels = latents.shape
     wide = -(-(cells + 1) // 16) * 16
     vmem = pl.BlockSpec(memory_space=pltpu.VMEM)
-    hbm = pl.BlockSpec(memory_space=pl.ANY)
+    hbm = pl.BlockSpec(memory_space=pltpu.HBM)
     bf16 = jnp.bfloat16
     dma = pltpu.SemaphoreType.DMA
-    row = lambda v: v.reshape(1, channels)
     taps = lambda k: k.reshape(9, 3 * channels, channels)
     return pl.pallas_call(
         functools.partial(kernel, tm_size, height_size),
         out_shape=jax.ShapeDtypeStruct(latents.shape, bf16),
         in_specs=[hbm, vmem, vmem, vmem, vmem, hbm, hbm],
-        out_specs=hbm,
+        out_specs=vmem,
         scratch_shapes=[
             pltpu.VMEM(latents.shape, bf16),
             pltpu.VMEM((9, 3 * channels, channels), bf16),
@@ -317,15 +310,14 @@
             pltpu.VMEM((rows, 2, cells, channels), bf16),
             pltpu.VMEM((2, 4, rows + 2, wide, 3 * channels), bf16),
             pltpu.VMEM((2, 2, rows, wide, channels), F32),
-            pltpu.VMEM(latents.shape, bf16),
-            dma((3,)), dma((rows,)),
+            dma((3,)),
             dma((2, rows)), dma((2, rows)),
             dma((2, 2)), dma((2, 2)), dma((2, 2)), dma((2, 2)),
         ],
         compiler_params=pltpu.CompilerParams(
             collective_id=0, has_side_effects=True, vmem_limit_bytes=60 * 1024 * 1024),
         name="residual_block",
-    )(latents, row(first_gain), row(second_gain), row(first_bias), row(second_bias),
+    )(latents, first_gain, second_gain, first_bias, second_bias,
       taps(first_kernel), taps(second_kernel))
 
 

time: 53.8 us -> 49.2 us (0.914)
  local copies, waits for them, and re-layouts: 6.99 us -> 2.11 us
    reshape x4 -> x0, local copies, waits for them, and re-layouts: 4.88 us -> none  [per_device(): row = lambda v: v.reshape(1, channels)]
where the time goes in v2:
time: 49.2 us; the launch traced here: 48.6 us
  Pallas kernels  46.5 us (95%)
  local copies, waits for them, and re-layouts  2.11 us (4%)
    pallas_call x1, Pallas kernels, per_device(): pl.pallas_call(functools.partial(kernel, tm_size, height_size), out_shape...  46.5 us
    unnamed x1, local copies, waits for them, and re-layouts  2.11 us

profile of v2, /device:TPU:225, one launch (start us, length us, event | category | flops | bytes accessed | tf_op | source)
XLA Modules:
  0.0 48.6 jit_solution(7137361334554079806)
XLA Ops:
  0.0 46.5 %residual_block.1 = bf16[2,8,104,256]{3,2,1,0:T(8,128)(2,1)} custom-call(bf16[2,8,104,256]{3,2,1,0:T(8,128)(2,1)} %lat.1, bf16[256]{0:T(256)(128)(2,1)} %gain1.1, bf16[256]{0:T(256)(128)(2,1)} %gain2.1, bf16[256]{0:T(256)(128)(2,1)} %bias1.1, bf16[256]{0:T(256)(128)(2,1)} %bias2.1, bf16[9,768,256]{2,1,0:T(8,128)(2,1)} %bitcast.2, bf16[9,768,256]{2,1,0:T(8,128)(2,1)} %bitcast.3), custom_call_target="tpu_custom_call" | custom-call | tf_op jit(solution)/shard_map/residual_block/pallas_call | solution.py:299
  46.5 2.1 %copy.9 = bf16[2,8,104,256]{3,2,1,0:T(8,128)(2,1)} copy(bf16[2,8,104,256]{3,2,1,0:T(8,128)(2,1)} %residual_block.1) | data formatting | bytes 1703936

commit v3 on v2

--- a/solution.py
+++ b/solution.py
@@ -10,14 +10,16 @@
 EPSILON = 1e-06
 MESH = pl.DeviceIdType.MESH
 F32 = jnp.float32
+RING = 4
+DETOURS = 2
 
 
 def kernel(
     tm_size, height_size,
     lat, gain1, gain2, bias1, bias2, w1_hbm, w2_hbm,
     out,
-    latv, w1, w2, halo, ledge, sendbuf, lhs, acc,
-    load_sem, tm_send, tm_recv, hl_send, hl_recv, hf_send, hf_recv,
+    latv, w1, w2, halo, ledge, sendbuf, lhs, acc, relay,
+    load_sem, tm_send, tm_recv, hl_send, hl_recv, hf_send, hf_recv, relay_send, relay_recv,
 ):
     frames, rows, cells, channels = latv.shape
     wide = lhs.shape[3]
@@ -37,18 +39,35 @@
 
     nxt = jnp.minimum(tm + 1, tm_size - 1)
     prv = jnp.maximum(tm - 1, 0)
+    x = lax.rem(tm, RING)
+    base = tm - x
+    left = base + lax.rem(x + RING - 1, RING)
+    right = base + lax.rem(x + 1, RING)
+    right2 = base + lax.rem(x + 2, RING)
+    crosses = (x == RING - 1) & has_next
+    crossed = (x == 0) & has_prev
+    relays_over = (x == 1) & (tm + 3 < tm_size)
     up = jnp.maximum(ht - 1, 0)
     down = jnp.minimum(ht + 1, height_size - 1)
 
     barrier = pltpu.get_barrier_semaphore()
     for exists, there in (
-        (has_prev, {"tm": prv}), (has_next, {"tm": nxt}),
+        (None, {"tm": left}), (None, {"tm": right}),
+        (crosses, {"tm": nxt}), (crossed, {"tm": prv}),
+        (relays_over, {"tm": jnp.minimum(tm + 3, tm_size - 1)}),
+        (crossed, {"tm": jnp.maximum(tm - 3, 0)}),
         (has_up, {"height": up}), (has_down, {"height": down}),
     ):
+        if exists is None:
+            pl.semaphore_signal(barrier, inc=1, device_id=there, device_id_type=MESH)
+            continue
+
         @pl.when(exists)
         def _(there=there):
             pl.semaphore_signal(barrier, inc=1, device_id=there, device_id_type=MESH)
-    peers = sum(h.astype(jnp.int32) for h in (has_prev, has_next, has_up, has_down))
+    peers = 2 + sum(
+        h.astype(jnp.int32)
+        for h in (crosses, crossed, relays_over, crossed, has_up, has_down))
     pl.semaphore_wait(barrier, peers)
 
     def source(e, row):
@@ -59,6 +78,33 @@
             src_ref=source(e, row), dst_ref=halo.at[e, row + 1],
             send_sem=tm_send.at[e, row], recv_sem=tm_recv.at[e, row],
             device_id={"tm": nxt}, device_id_type=MESH)
+
+    def detour_row(e, k):
+        return (rows - 3 if e == 0 else 0) + k
+
+    def hop_copy(hop, e, k):
+        row = detour_row(e, k)
+        last = hop == 2
+        return pltpu.make_async_remote_copy(
+            src_ref=source(e, row) if hop == 0 else relay.at[hop - 1, e, k],
+            dst_ref=halo.at[e, row + 1] if last else relay.at[hop, e, k],
+            send_sem=relay_send.at[hop, e, k],
+            recv_sem=tm_recv.at[e, row] if last else relay_recv.at[hop, e, k],
+            device_id={"tm": jnp.minimum(right2 + 1, tm_size - 1) if last else left},
+            device_id_type=MESH)
+
+    hop_runs = (has_next, right < tm_size - 1, right2 < tm_size - 1)
+
+    def start_detour(e, k):
+        @pl.when(hop_runs[0])
+        def _():
+            hop_copy(0, e, k).start()
+
+    def pass_on(hop, e, k):
+        @pl.when(hop_runs[hop])
+        def _():
+            hop_copy(hop - 1, e, k).wait_recv()
+            hop_copy(hop, e, k).start()
 
     def local_edge(e, side):
         return pltpu.make_async_remote_copy(
@@ -86,6 +132,8 @@
         def _():
             local_edge(e, side).start()
 
+    for k in range(DETOURS):
+        start_detour(0, k)
     start_local_edge(0, 0)
     start_local_edge(0, 1)
 
@@ -93,7 +141,7 @@
         start_tm(0, lax.rem(i + rows - 1, rows))
         return carry
 
-    lax.fori_loop(0, rows, send_row, 0)
+    lax.fori_loop(0, rows - DETOURS, send_row, 0)
 
     g1 = gain1[...].astype(F32).reshape(1, channels)
     g2 = gain2[...].astype(F32).reshape(1, channels)
@@ -177,6 +225,7 @@
     def local_conv(e, w, count):
         def chunk(c, carry):
             row = c * count
+            pass_on(1 + e, e, c)
             first = sum(tap(e, w, 2, row, count, 2, j) for j in range(3))
             acc[e, 0, pl.ds(row, count)] = first.reshape(count, wide, channels)
             second = sum(
@@ -214,26 +263,56 @@
     take_halo(0, 0)
     take_halo_edge(0, 0)
     take_halo_edge(0, 1)
+    pass_on(2, 0, 0)
 
     def middle_step(r, carry):
         take_halo(0, r)
         middle_row(r - 1)
 
-        @pl.when(r > 1)
+        @pl.when(r == 1)
+        def _():
+            pass_on(2, 0, 1)
+
+        @pl.when(r == 2)
+        def _():
+            start_detour(1, 0)
+            start_local_edge(1, 0)
+
+        @pl.when(r == 3)
+        def _():
+            start_detour(1, 1)
+
+        @pl.when(r > 3)
         def _():
             start_tm(1, r - 2)
         return carry
 
-    lax.fori_loop(1, rows - 2, middle_step, 0)
-    start_local_edge(1, 0)
+    lax.fori_loop(1, rows - 3, middle_step, 0)
+    take_halo(0, rows - 3)
+    start_tm(1, rows - 5)
+    pass_on(1, 1, 0)
     take_halo(0, rows - 2)
-    start_tm(1, rows - 4)
-    middle_row(rows - 1)
-    middle_row(rows - 3)
-    start_tm(1, rows - 1)
-    start_local_edge(1, 1)
-    middle_row(rows - 2)
-    start_tm(1, rows - 3)
+
+    def late_row(i):
+        return rows - 4 + lax.rem(i + 3, 4)
+
+    def late_step(i, carry):
+        middle_row(late_row(i))
+
+        @pl.when(i == 0)
+        def _():
+            pass_on(1, 1, 1)
+
+        @pl.when(i == 1)
+        def _():
+            start_local_edge(1, 1)
+
+        @pl.when(i > 0)
+        def _():
+            start_tm(1, late_row(i - 1 + 4))
+        return carry
+
+    lax.fori_loop(0, 4, late_step, 0)
     take_local_edge(1, 0)
     start_tm(1, rows - 2)
     take_local_edge(1, 1)
@@ -244,36 +323,43 @@
         for f, v in enumerate(halo_conv(1, w2, row)):
             out[f, row] = (latv[f, row].astype(F32) + (v + b2)).astype(jnp.bfloat16)
 
+    def last_rows(first, count, step):
+        def body(i, carry):
+            last_row(first + step * i)
+            return carry
+        lax.fori_loop(0, count, body, 0)
+
+    take_halo(1, 2)
+    take_halo(1, 3)
+    take_halo(1, rows - 1)
     take_halo(1, 0)
-
-    def last_step(r, carry):
-        take_halo(1, r)
-
-        @pl.when(r > 1)
-        def _():
-            last_row(r - 1)
-        return carry
-
-    lax.fori_loop(1, rows - 3, last_step, 0)
-    take_halo(1, rows - 1)
-    take_halo(1, rows - 3)
-    last_row(rows - 4)
+    take_halo(1, 4)
+    last_row(3)
+    take_halo(1, 1)
+    last_rows(2, 2, -1)
+    take_halo(1, 5)
+    last_row(4)
     take_halo_edge(1, 1)
     last_row(0)
     take_halo_edge(1, 0)
-    take_halo(1, rows - 2)
-    last_row(rows - 3)
-    last_row(rows - 2)
-    last_row(rows - 1)
-
-    def drain(row, carry):
+    take_halo(1, 6)
+    last_rows(5, 3, 1)
+
+    def drain(i, carry):
         @pl.when(has_next)
         def _():
-            tm_copy(0, row).wait_send()
-            tm_copy(1, row).wait_send()
+            tm_copy(0, lax.rem(i + rows - 1, rows)).wait_send()
+            tm_copy(1, i + DETOURS).wait_send()
         return carry
 
-    lax.fori_loop(0, rows, drain, 0)
+    lax.fori_loop(0, rows - DETOURS, drain, 0)
+    for hop in range(3):
+        @pl.when(hop_runs[hop])
+        def _(hop=hop):
+            for e in range(2):
+                for k in range(DETOURS):
+                    hop_copy(hop, e, k).wait_send()
+
     for e in range(2):
         for side in range(2):
             @pl.when(to_side[side])
@@ -310,9 +396,11 @@
             pltpu.VMEM((rows, 2, cells, channels), bf16),
             pltpu.VMEM((2, 4, rows + 2, wide, 3 * channels), bf16),
             pltpu.VMEM((2, 2, rows, wide, channels), F32),
+            pltpu.VMEM((2, 2, DETOURS, 2, cells, channels), bf16),
             dma((3,)),
             dma((2, rows)), dma((2, rows)),
             dma((2, 2)), dma((2, 2)), dma((2, 2)), dma((2, 2)),
+            dma((3, 2, DETOURS)), dma((2, 2, DETOURS)),
         ],
         compiler_params=pltpu.CompilerParams(
             collective_id=0, has_side_effects=True, vmem_limit_bytes=60 * 1024 * 1024),

time: 49.2 us -> 47 us (0.955)
  Pallas kernels: 46.5 us -> 44 us
    pallas_call x1, Pallas kernels: 46.5 us -> 44 us  [per_device(): pl.pallas_call(functools.partial(kernel, tm_size, height_size), out_shape...]
where the time goes in v3:
time: 47 us; the launch traced here: 46.1 us
  Pallas kernels  44 us (94%)
  local copies, waits for them, and re-layouts  2.11 us (4%)
    pallas_call x1, Pallas kernels, per_device(): pl.pallas_call(functools.partial(kernel, tm_size, height_size), out_shape...  44 us
    unnamed x1, local copies, waits for them, and re-layouts  2.11 us

profile of v3, /device:TPU:225, one launch (start us, length us, event | category | flops | bytes accessed | tf_op | source)
XLA Modules:
  0.0 46.1 jit_solution(4022876845552185532)
XLA Ops:
  0.0 44.0 %residual_block.1 = bf16[2,8,104,256]{3,2,1,0:T(8,128)(2,1)} custom-call(bf16[2,8,104,256]{3,2,1,0:T(8,128)(2,1)} %lat.1, bf16[256]{0:T(256)(128)(2,1)} %gain1.1, bf16[256]{0:T(256)(128)(2,1)} %gain2.1, bf16[256]{0:T(256)(128)(2,1)} %bias1.1, bf16[256]{0:T(256)(128)(2,1)} %bias2.1, bf16[9,768,256]{2,1,0:T(8,128)(2,1)} %bitcast.2, bf16[9,768,256]{2,1,0:T(8,128)(2,1)} %bitcast.3), custom_call_target="tpu_custom_call" | custom-call | tf_op jit(solution)/shard_map/residual_block/pallas_call | solution.py:385
  44.0 2.1 %copy.9 = bf16[2,8,104,256]{3,2,1,0:T(8,128)(2,1)} copy(bf16[2,8,104,256]{3,2,1,0:T(8,128)(2,1)} %residual_block.1) | data formatting | bytes 1703936

commit v4 on v3

--- a/solution.py
+++ b/solution.py
@@ -234,11 +234,18 @@
             return carry
         lax.fori_loop(0, rows // count, chunk, 0)
 
-    def halo_conv(e, w, row):
-        first = acc[e, 0, row] + sum(
-            tap(e, w, 0, row, 1, 0, j) + tap(e, w, 1, row, 1, 1, j) for j in range(3))
-        second = acc[e, 1, row] + sum(tap(e, w, 1, row, 1, 0, j) for j in range(3))
-        return first[:cells], second[:cells]
+    def halo_conv(e, w, row, count):
+        shape = (count, wide, channels)
+
+        def both(j):
+            block = lhs[e, 0:2, pl.ds(row + j, count)].reshape(2 * count * wide, 3 * channels)
+            return jnp.dot(block, w[j], preferred_element_type=F32)
+
+        pair = sum(both(j) for j in range(3)).reshape(2, *shape)
+        middle = sum(tap(e, w, 1, row, count, 1, j) for j in range(3)).reshape(shape)
+        first = acc[e, 0, pl.ds(row, count)] + pair[0] + middle
+        second = acc[e, 1, pl.ds(row, count)] + pair[1]
+        return first[:, :cells], second[:, :cells]
 
     load_lat.wait()
 
@@ -253,11 +260,12 @@
     load_w1.wait()
     local_conv(0, w1, 4)
 
-    def middle_row(row):
-        for f, v in enumerate(halo_conv(0, w1, row)):
-            a = activate((v + b1).astype(jnp.bfloat16).astype(F32), g2)
-            sendbuf[row, f] = a.astype(jnp.bfloat16)
-            expand(1, 2 + f, row + 1, a)
+    def middle_rows(row, count):
+        for f, v in enumerate(halo_conv(0, w1, row, count)):
+            for c in range(count):
+                a = activate((v[c] + b1).astype(jnp.bfloat16).astype(F32), g2)
+                sendbuf[row + c, f] = a.astype(jnp.bfloat16)
+                expand(1, 2 + f, row + c + 1, a)
 
     take_halo(0, rows - 1)
     take_halo(0, 0)
@@ -267,7 +275,7 @@
 
     def middle_step(r, carry):
         take_halo(0, r)
-        middle_row(r - 1)
+        middle_rows(r - 1, 1)
 
         @pl.when(r == 1)
         def _():
@@ -293,57 +301,39 @@
     pass_on(1, 1, 0)
     take_halo(0, rows - 2)
 
-    def late_row(i):
-        return rows - 4 + lax.rem(i + 3, 4)
-
-    def late_step(i, carry):
-        middle_row(late_row(i))
-
-        @pl.when(i == 0)
-        def _():
-            pass_on(1, 1, 1)
-
-        @pl.when(i == 1)
-        def _():
-            start_local_edge(1, 1)
-
-        @pl.when(i > 0)
-        def _():
-            start_tm(1, late_row(i - 1 + 4))
-        return carry
-
-    lax.fori_loop(0, 4, late_step, 0)
+    middle_rows(rows - 2, 2)
+    pass_on(1, 1, 1)
     take_local_edge(1, 0)
+    start_tm(1, rows - 1)
+    start_local_edge(1, 1)
     start_tm(1, rows - 2)
+    middle_rows(rows - 4, 2)
     take_local_edge(1, 1)
+    start_tm(1, rows - 3)
+    start_tm(1, rows - 4)
     load_w2.wait()
     local_conv(1, w2, 4)
 
-    def last_row(row):
-        for f, v in enumerate(halo_conv(1, w2, row)):
-            out[f, row] = (latv[f, row].astype(F32) + (v + b2)).astype(jnp.bfloat16)
-
-    def last_rows(first, count, step):
-        def body(i, carry):
-            last_row(first + step * i)
-            return carry
-        lax.fori_loop(0, count, body, 0)
+    def last_rows(row, count):
+        for f, v in enumerate(halo_conv(1, w2, row, count)):
+            for c in range(count):
+                out[f, row + c] = (
+                    latv[f, row + c].astype(F32) + (v[c] + b2)).astype(jnp.bfloat16)
 
     take_halo(1, 2)
     take_halo(1, 3)
     take_halo(1, rows - 1)
     take_halo(1, 0)
+    take_halo(1, 1)
+    last_rows(1, 2)
+    take_halo_edge(1, 1)
+    last_rows(0, 1)
+    take_halo(1, 6)
+    take_halo_edge(1, 0)
+    take_halo(1, 5)
+    last_rows(6, 2)
     take_halo(1, 4)
-    last_row(3)
-    take_halo(1, 1)
-    last_rows(2, 2, -1)
-    take_halo(1, 5)
-    last_row(4)
-    take_halo_edge(1, 1)
-    last_row(0)
-    take_halo_edge(1, 0)
-    take_halo(1, 6)
-    last_rows(5, 3, 1)
+    last_rows(3, 3)
 
     def drain(i, carry):
         @pl.when(has_next)

time: 47 us -> 49.4 us (1.051)
  the two profiles are of different devices: /device:TPU:225 before, /device:TPU:126 now
where the time goes in v4:
time: 49.4 us; the launch traced here: 49.3 us
  Pallas kernels  47.1 us (95%)
  local copies, waits for them, and re-layouts  2.11 us (4%)
    pallas_call x1, Pallas kernels, per_device(): pl.pallas_call(functools.partial(kernel, tm_size, height_size), out_shape...  47.1 us
    unnamed x1, local copies, waits for them, and re-layouts  2.11 us

profile of v4, /device:TPU:126, one launch (start us, length us, event | category | flops | bytes accessed | tf_op | source)
XLA Modules:
  0.0 49.3 jit_solution(3837961924967256043)
XLA Ops:
  0.0 47.1 %residual_block.1 = bf16[2,8,104,256]{3,2,1,0:T(8,128)(2,1)} custom-call(bf16[2,8,104,256]{3,2,1,0:T(8,128)(2,1)} %lat.1, bf16[256]{0:T(256)(128)(2,1)} %gain1.1, bf16[256]{0:T(256)(128)(2,1)} %gain2.1, bf16[256]{0:T(256)(128)(2,1)} %bias1.1, bf16[256]{0:T(256)(128)(2,1)} %bias2.1, bf16[9,768,256]{2,1,0:T(8,128)(2,1)} %bitcast.2, bf16[9,768,256]{2,1,0:T(8,128)(2,1)} %bitcast.3), custom_call_target="tpu_custom_call" | custom-call | tf_op jit(solution)/shard_map/residual_block/pallas_call | solution.py:375
  47.2 2.1 %copy.9 = bf16[2,8,104,256]{3,2,1,0:T(8,128)(2,1)} copy(bf16[2,8,104,256]{3,2,1,0:T(8,128)(2,1)} %residual_block.1) | data formatting | bytes 1703936

commit v5 on v3

--- a/solution.py
+++ b/solution.py
@@ -11,7 +11,7 @@
 MESH = pl.DeviceIdType.MESH
 F32 = jnp.float32
 RING = 4
-DETOURS = 2
+DETOURS = (2, 1)
 
 
 def kernel(
@@ -132,7 +132,7 @@
         def _():
             local_edge(e, side).start()
 
-    for k in range(DETOURS):
+    for k in range(DETOURS[0]):
         start_detour(0, k)
     start_local_edge(0, 0)
     start_local_edge(0, 1)
@@ -141,7 +141,7 @@
         start_tm(0, lax.rem(i + rows - 1, rows))
         return carry
 
-    lax.fori_loop(0, rows - DETOURS, send_row, 0)
+    lax.fori_loop(0, rows - DETOURS[0], send_row, 0)
 
     g1 = gain1[...].astype(F32).reshape(1, channels)
     g2 = gain2[...].astype(F32).reshape(1, channels)
@@ -225,7 +225,8 @@
     def local_conv(e, w, count):
         def chunk(c, carry):
             row = c * count
-            pass_on(1 + e, e, c)
+            if e == 0:
+                pass_on(1, 0, c)
             first = sum(tap(e, w, 2, row, count, 2, j) for j in range(3))
             acc[e, 0, pl.ds(row, count)] = first.reshape(count, wide, channels)
             second = sum(
@@ -280,7 +281,7 @@
 
         @pl.when(r == 3)
         def _():
-            start_detour(1, 1)
+            start_tm(1, 1)
 
         @pl.when(r > 3)
         def _():
@@ -299,10 +300,6 @@
     def late_step(i, carry):
         middle_row(late_row(i))
 
-        @pl.when(i == 0)
-        def _():
-            pass_on(1, 1, 1)
-
         @pl.when(i == 1)
         def _():
             start_local_edge(1, 1)
@@ -317,6 +314,7 @@
     start_tm(1, rows - 2)
     take_local_edge(1, 1)
     load_w2.wait()
+    pass_on(2, 1, 0)
     local_conv(1, w2, 4)
 
     def last_row(row):
@@ -329,16 +327,16 @@
             return carry
         lax.fori_loop(0, count, body, 0)
 
+    take_halo(1, 1)
     take_halo(1, 2)
     take_halo(1, 3)
+    last_row(2)
     take_halo(1, rows - 1)
-    take_halo(1, 0)
     take_halo(1, 4)
     last_row(3)
-    take_halo(1, 1)
-    last_rows(2, 2, -1)
+    take_halo(1, 0)
     take_halo(1, 5)
-    last_row(4)
+    last_rows(4, 2, -3)
     take_halo_edge(1, 1)
     last_row(0)
     take_halo_edge(1, 0)
@@ -349,15 +347,20 @@
         @pl.when(has_next)
         def _():
             tm_copy(0, lax.rem(i + rows - 1, rows)).wait_send()
-            tm_copy(1, i + DETOURS).wait_send()
+            tm_copy(1, i + 1).wait_send()
         return carry
 
-    lax.fori_loop(0, rows - DETOURS, drain, 0)
+    lax.fori_loop(0, rows - DETOURS[0], drain, 0)
+
+    @pl.when(has_next)
+    def _():
+        tm_copy(1, rows - 1).wait_send()
+
     for hop in range(3):
         @pl.when(hop_runs[hop])
         def _(hop=hop):
             for e in range(2):
-                for k in range(DETOURS):
+                for k in range(DETOURS[e]):
                     hop_copy(hop, e, k).wait_send()
 
     for e in range(2):
@@ -396,11 +399,11 @@
             pltpu.VMEM((rows, 2, cells, channels), bf16),
             pltpu.VMEM((2, 4, rows + 2, wide, 3 * channels), bf16),
             pltpu.VMEM((2, 2, rows, wide, channels), F32),
-            pltpu.VMEM((2, 2, DETOURS, 2, cells, channels), bf16),
+            pltpu.VMEM((2, 2, DETOURS[0], 2, cells, channels), bf16),
             dma((3,)),
             dma((2, rows)), dma((2, rows)),
             dma((2, 2)), dma((2, 2)), dma((2, 2)), dma((2, 2)),
-            dma((3, 2, DETOURS)), dma((2, 2, DETOURS)),
+            dma((3, 2, DETOURS[0])), dma((2, 2, DETOURS[0])),
         ],
         compiler_params=pltpu.CompilerParams(
             collective_id=0, has_side_effects=True, vmem_limit_bytes=60 * 1024 * 1024),

time: 47 us -> 45.6 us (0.970); the launches traced: 46.1 us -> 45.5 us
  Pallas kernels: 44 us -> 43.4 us
    pallas_call x1, Pallas kernels: 44 us -> 43.4 us  [per_device(): pl.pallas_call(functools.partial(kernel, tm_size, height_size), out_shape...]
where the time goes in v5:
time: 45.6 us; the launch traced here: 45.5 us
  Pallas kernels  43.4 us (95%)
  local copies, waits for them, and re-layouts  2.11 us (5%)
    pallas_call x1, Pallas kernels, per_device(): pl.pallas_call(functools.partial(kernel, tm_size, height_size), out_shape...  43.4 us
    unnamed x1, local copies, waits for them, and re-layouts  2.11 us

profile of v5, /device:TPU:225, one launch (start us, length us, event | category | flops | bytes accessed | tf_op | source)
XLA Modules:
  0.0 45.5 jit_solution(10215630467704335702)
XLA Ops:
  0.0 43.4 %residual_block.1 = bf16[2,8,104,256]{3,2,1,0:T(8,128)(2,1)} custom-call(bf16[2,8,104,256]{3,2,1,0:T(8,128)(2,1)} %lat.1, bf16[256]{0:T(256)(128)(2,1)} %gain1.1, bf16[256]{0:T(256)(128)(2,1)} %gain2.1, bf16[256]{0:T(256)(128)(2,1)} %bias1.1, bf16[256]{0:T(256)(128)(2,1)} %bias2.1, bf16[9,768,256]{2,1,0:T(8,128)(2,1)} %bitcast.2, bf16[9,768,256]{2,1,0:T(8,128)(2,1)} %bitcast.3), custom_call_target="tpu_custom_call" | custom-call | tf_op jit(solution)/shard_map/residual_block/pallas_call | solution.py:388
  43.4 2.1 %copy.9 = bf16[2,8,104,256]{3,2,1,0:T(8,128)(2,1)} copy(bf16[2,8,104,256]{3,2,1,0:T(8,128)(2,1)} %residual_block.1) | data formatting | bytes 1703936
